TPU v7x, 512 devices: a whole 4x8x8 slice. The times are simulated.
512 devices in a mesh: seq: 128 (over y, z, core), head: 4 (over x).
Axes of the slice: x: 4, y: 8, z: 8, core: 2. Of those that a mesh axis runs over, the one named last changes fastest.
Arguments:
- queries: bfloat16 [65536, 2048], P('seq', 'head'), may hold values from -4 to 4
- keys: bfloat16 [65536, 2048], P('seq', 'head'), may hold values from -4 to 4
- values: bfloat16 [65536, 2048], P('seq', 'head'), may hold values from -6 to 6
- rates: float32 [65536, 4], P('seq', 'head'), may hold values from 0.02 to 0.3
- fast: bfloat16 [4, 3, 512, 512], P('head'), may hold values from -0.25 to 0.25
- momentum: float32 [4, 3, 512, 512], P('head', None, 'seq'), may hold values from -0.24 to 0.24
- out_proj: bfloat16 [2048, 2048], P('seq', 'head'), may hold values from -0.125 to 0.125
Outputs:
- mixed: bfloat16 [65536, 2048], P('seq', 'head')
- new_momentum: float32 [4, 3, 512, 512], P('head', None, 'seq')
All inputs are finite; a program needn't handle non-finite values.
Results may differ from a plain program's by a relative error of at most 0.0094.
Values may be sent and summed in bfloat16 or wider, within the bound.
A program may use at most 64 MiB of HBM per device.

v0:
```python
import math
import jax
import jax.numpy as jnp
from jax import lax
from jax.sharding import PartitionSpec as P

HD = 512
WINDOW = 512
MOMENTUM_DECAY = 0.9
NORM_EPS = 1e-06
NEG_LARGE = -1e30


def from_behind(array, axis, by):
    devices = lax.axis_size(axis)
    pairs = [(i, i + by) for i in range(devices) if 0 <= i + by < devices]
    return lax.ppermute(array, axis, pairs)


def times_transposed(left, right):
    return lax.dot_general(
        left, right, (((1,), (1,)), ((), ())), preferred_element_type=jnp.float32
    )


def contract_rows(left, right):
    return lax.dot_general(
        left, right, (((0,), (0,)), ((), ())), preferred_element_type=jnp.float32
    )


def renormalize(base, moment):
    updated = base - moment
    base_rms = jnp.sqrt(jnp.mean(base * base, axis=-1, keepdims=True) + NORM_EPS)
    new_rms = jnp.sqrt(jnp.mean(updated * updated, axis=-1, keepdims=True) + NORM_EPS)
    return (updated * (base_rms / new_rms)).astype(jnp.bfloat16)


def shards(queries, keys, values, rates, fast, momentum, out_proj):
    tok_rows = queries.shape[0]
    ranks = lax.axis_size("seq")
    position = lax.axis_index("seq")
    own_rows = momentum.shape[2]
    grad_scale = 1.0 / math.sqrt(tok_rows * ranks)
    weights = fast[0]
    h_gate = times_transposed(keys, weights[0])
    h_up = times_transposed(keys, weights[1])
    sigma = jax.nn.sigmoid(h_gate)
    gated = (h_gate * sigma * h_up).astype(jnp.bfloat16)
    errors = (-grad_scale * rates * values.astype(jnp.float32)).astype(jnp.bfloat16)
    grad_down = contract_rows(errors, gated)
    back = jnp.dot(errors, weights[2], preferred_element_type=jnp.float32)
    d_gate = (back * h_up * sigma * (1.0 + h_gate * (1.0 - sigma))).astype(jnp.bfloat16)
    d_up = (back * h_gate * sigma).astype(jnp.bfloat16)
    grad_gate = contract_rows(d_gate, keys)
    grad_up = contract_rows(d_up, keys)
    grads = jnp.stack([grad_gate, grad_up, grad_down])
    row_start = position * own_rows
    placed = lax.dynamic_update_slice_in_dim(
        jnp.zeros(grads.shape, jnp.float32), MOMENTUM_DECAY * momentum[0], row_start, 1
    )
    moment_full = lax.psum(grads + placed, "seq")
    renewed = renormalize(weights.astype(jnp.float32), moment_full)
    moment_own = lax.dynamic_slice_in_dim(moment_full, row_start, own_rows, 1)
    q_gate = times_transposed(queries, renewed[0])
    q_up = times_transposed(queries, renewed[1])
    fast_in = (q_gate * jax.nn.sigmoid(q_gate) * q_up).astype(jnp.bfloat16)
    fast_out = times_transposed(fast_in, renewed[2])
    reach = (WINDOW + tok_rows - 2) // tok_rows
    stacked = jnp.stack([keys, values])
    earlier = [from_behind(stacked, "seq", 1)]
    extended = jnp.concatenate(earlier + [stacked], axis=1)
    key_count = extended.shape[1]
    key_pos = (position - reach) * tok_rows + jnp.arange(key_count)
    block = min(512, tok_rows)
    query_pos = position * tok_rows + 0 + jnp.arange(block)
    spacing = query_pos[:, None] - key_pos[None, :]
    allowed = (spacing >= 0) & (spacing < WINDOW) & (key_pos[None, :] >= 0)
    scores = times_transposed(queries, extended[0]) * (1.0 / math.sqrt(HD))
    scores = jnp.where(allowed, scores, NEG_LARGE)
    highest = jnp.max(scores, axis=1, keepdims=True)
    expo = jnp.exp(scores - highest)
    probs = (expo / jnp.sum(expo, axis=1, keepdims=True)).astype(jnp.bfloat16)
    attended_parts = jnp.dot(probs, extended[1], preferred_element_type=jnp.float32)
    combined = (attended_parts + fast_out).astype(jnp.bfloat16)
    all_heads = lax.all_gather(combined, "head", axis=1, tiled=True)
    projected = jnp.dot(
        all_heads,
        lax.all_gather(out_proj, "seq", axis=0, tiled=True),
        preferred_element_type=jnp.float32,
    )
    return (projected.astype(jnp.bfloat16), moment_own[None])


def solution(mesh):
    return jax.shard_map(
        shards,
        mesh=mesh,
        in_specs=(
            P("seq", "head"),
            P("seq", "head"),
            P("seq", "head"),
            P("seq", "head"),
            P("head", None, None, None),
            P("head", None, "seq", None),
            P("seq", "head"),
        ),
        out_specs=(P("seq", "head"), P("head", None, "seq", None)),
        check_vma=False,
    )
```

profile of v0, /device:TPU:1, one launch (start us, length us, event | category | flops | bytes accessed | tf_op | source)
XLA Modules:
  0.0 359.7 jit_solution(3982330911854318718)
XLA Ops:
  7.2 0.0 copy-start
  7.2 0.0 copy-start.1
  7.2 0.0 copy-start.3
  7.2 0.0 all-reduce.2.cloned.1.call-start
  7.2 0.0 copy-start.10
  7.3 0.0 copy-start.4
  7.3 1.8 fusion.14
  9.1 0.0 copy-done.1
  9.1 0.0 copy-done.3
  9.1 0.5 fusion.16
  9.6 0.0 copy-done.10
  9.6 0.0 copy-done.4
  9.6 0.5 fusion.18
  10.1 1.6 convolution_bitcast_fusion.2
  11.7 1.8 convolution_bitcast_fusion.4
  13.5 1.5 convolution_bitcast_fusion.3
  15.0 3.9 %pad_maximum_fusion = f32[3,512,512]{2,1,0:T(8,128)} fusion(f32[1,512,512]{2,1,0:T(8,128)} %convolution_bitcast_fusion.2, f32[1,512,512]{2,1,0:T(8,128)} %convolution_bitcast_fusion.3, f32[1,512,512]{2,1,0:T(8,128)} %convolution_bitcast_fusion.4), kind=kLoop, calls=%fused_computation.3 | loop fusion | flops 1572864 | bytes 6291456 | tf_op jit(solution)/shard_map/stack | solution.py:57
  18.9 0.0 copy-done.9
  18.9 1.4 fusion.26
  20.3 0.0 all-reduce.2.cloned.1.call-update
  20.3 0.0 all-gather.5.cloned.1.call-start
  20.4 0.7 all-gather.5.cloned.1.call-update
  21.1 0.0 all-gather.3.cloned.1.call-start
  21.1 1.2 pad_maximum_fusion.1
  22.3 5.4 %collective-permute-start = (bf16[2,512,512]{2,1,0:T(8,128)(2,1)}, bf16[2,512,512]{2,1,0:T(8,128)(2,1)}, u32[]{:S(2)}, u32[]{:S(2)}) collective-permute-start(bf16[2,512,512]{2,1,0:T(8,128)(2,1)} %pad_maximum_fusion.1), channel_id=1, source_target_pairs={{0,4},{4,8},{8,12},{12,16},{16,20},{20,24},{24,28},{28,32},{32,36}... | collective-permute-start | bytes 3145736 | tf_op jit(solution)/shard_map/ppermute | solution.py:17
  27.7 12.2 %collective-permute-done = bf16[2,512,512]{2,1,0:T(8,128)(2,1)} collective-permute-done((bf16[2,512,512]{2,1,0:T(8,128)(2,1)}, bf16[2,512,512]{2,1,0:T(8,128)(2,1)}, u32[]{:S(2)}, u32[]{:S(2)}) %collective-permute-start) | collective-permute-done | bytes 1048608 | tf_op jit(solution)/shard_map/ppermute | solution.py:17
  39.9 1.4 maximum_maximum_fusion
  41.3 0.0 copy-done
  41.3 0.0 copy-start.6
  41.3 1.1 fusion.31
  42.5 0.2 copy-done.6
  42.7 1.3 copy-done.8
  44.0 0.4 fusion.3
  44.4 185.0 %all-reduce.2.cloned.1.call-done = f32[3,512,512]{2,1,0:T(8,128)} async-done(((f32[3,512,512]{2,1,0:T(8,128)}), f32[3,512,512]{2,1,0:T(8,128)}) %all-reduce.2.cloned.1.call-update) | async-done | bytes 3145744 | tf_op jit(solution)/shard_map/psum | solution.py:62
  229.4 2.7 fusion
  232.2 0.1 copy-done.2
  232.3 0.4 multiply_convert_fusion
  232.7 0.0 copy-start.5
  232.7 1.2 copy-done.5
  233.8 1.5 convolution_bitcast_fusion.1
  235.3 3.5 fusion.7
  238.8 0.0 copy-done.7
  238.8 3.4 fusion.5
  242.2 0.0 all-gather.3.cloned.1.call-update
  242.2 1.4 dynamic-slice_bitcast_fusion
  243.7 70.2 %all-gather.5.cloned.1.call-done = bf16[2048,512]{1,0:T(8,128)(2,1)} async-done(((bf16[16,512]{1,0:T(8,128)(2,1)}), bf16[2048,512]{1,0:T(8,128)(2,1)}) %all-gather.5.cloned.1.call-update) | async-done | bytes 2097168 | tf_op jit(solution)/shard_map/all_gather | solution.py:89
  313.8 35.1 %all-gather.3.cloned.1.call-done = bf16[512,2048]{1,0:T(8,128)(2,1)} async-done(((bf16[512,512]{1,0:T(8,128)(2,1)}), bf16[512,2048]{1,0:T(8,128)(2,1)}) %all-gather.3.cloned.1.call-update) | async-done | bytes 2097168 | tf_op jit(solution)/shard_map/all_gather | solution.py:86
  348.9 4.3 %convolution_convert_fusion = bf16[512,512]{1,0:T(8,128)(2,1)} fusion(bf16[512,2048]{1,0:T(8,128)(2,1)} %all-gather.3.cloned.1.call-done, bf16[2048,512]{1,0:T(8,128)(2,1)} %all-gather.5.cloned.1.call-done), kind=kOutput, calls=%fused_computation.23 | convolution fusion | flops 1074003968 | bytes 4718592 | tf_op jit(solution)/shard_map/dot_general | solution.py:87
  (9 shorter events, 0.0 us)
Async XLA Ops:
  7.2 34.1 %copy-start = (bf16[512,512]{1,0:T(8,128)(2,1)S(1)}, bf16[512,512]{1,0:T(8,128)(2,1)}, u32[]{:S(2)}) copy-start(bf16[512,512]{1,0:T(8,128)(2,1)} %param.7) | copy-start | bytes 1572868
  7.2 1.9 copy-start.1
  7.2 1.9 copy-start.3
  7.2 222.2 %all-reduce.2.cloned.1.call-start = ((), (), s32[]{:S(2)}) async-start(), calls=%async_computation | async-start | bytes 6291456 | tf_op jit(solution)/shard_map/psum | solution.py:62
  7.2 2.3 copy-start.10
  7.3 2.3 copy-start.4
  15.0 3.9 %copy-start.9 = (f32[1,3,4,512]{3,2,1,0:T(4,128)S(1)}, f32[1,3,4,512]{3,2,1,0:T(4,128)}, u32[]{:S(2)}) copy-start(f32[1,3,4,512]{3,2,1,0:T(4,128)} %param.12) | copy-start | bytes 73732
  20.3 293.5 %all-gather.5.cloned.1.call-start = ((), (), s32[]{:S(2)}) async-start(), calls=%async_computation.2 | async-start | bytes 2113536 | tf_op jit(solution)/shard_map/all_gather | solution.py:89
  21.1 327.8 %all-gather.3.cloned.1.call-start = ((), (), s32[]{:S(2)}) async-start(), calls=%async_computation.1 | async-start | bytes 2621440 | tf_op jit(solution)/shard_map/all_gather | solution.py:86
  22.3 17.6 %collective-permute-start = (bf16[2,512,512]{2,1,0:T(8,128)(2,1)}, bf16[2,512,512]{2,1,0:T(8,128)(2,1)}, u32[]{:S(2)}, u32[]{:S(2)}) collective-permute-start(bf16[2,512,512]{2,1,0:T(8,128)(2,1)} %pad_maximum_fusion.1), channel_id=1, source_target_pairs={{0,4},{4,8},{8,12},{12,16},{16,20},{20,24},{24,28},{28,32},{32,36}... | collective-permute-start | bytes 3145736 | tf_op jit(solution)/shard_map/ppermute | solution.py:17
  41.3 1.4 copy-start.6
  42.7 1.3 copy-start.8
  229.4 2.8 copy-start.2
  232.7 1.2 copy-start.5
  235.3 3.5 copy-start.7
Sparse Core Ops, SparseCore 0:
  20.5 208.9 all-reduce.1
  232.5 81.2 all-gather.4
  316.5 32.3 all-gather.2
where the time goes:
time: 360 us
  waiting for transfers between devices  303 us (84%)
  matrix products  21.5 us (6%)
  between operations  13.9 us (4%)
  other arithmetic  11.3 us (3%)
  starting transfers between devices  5.49 us (2%)
  local copies, waits for them, and re-layouts  4.24 us (1%)
    psum x1, waiting for transfers between devices, shards(): moment_full = lax.psum(grads + placed, 'seq')  185 us
    all_gather x1, waiting for transfers between devices, shards(): lax.all_gather(out_proj, 'seq', axis=0, tiled=True)  70.2 us
    all_gather x1, waiting for transfers between devices, shards(): all_heads = lax.all_gather(combined, 'head', axis=1, tiled=True)  35.1 us
    ppermute x1, waiting for transfers between devices, from_behind(): return lax.ppermute(array, axis, pairs)  12.2 us
    dot_general x5, matrix products, times_transposed(): lax.dot_general(left, right, (((1,), (1,)), ((), ())), preferred_element_...  8.38 us
  transfers between devices with their start and end apart: 4, of which 4 were waited for; matrix products, arithmetic and copies ran while one was open for 5% of the time, Pallas kernels for 0%

commit v1 on v0

--- a/solution.py
+++ b/solution.py
@@ -86,7 +86,15 @@
     all_heads = lax.all_gather(combined, "head", axis=1, tiled=True)
     projected = jnp.dot(
         all_heads,
-        lax.all_gather(out_proj, "seq", axis=0, tiled=True),
+        jnp.concatenate(
+            lax.all_to_all(
+                jnp.stack(lax.psum(1, axis_name="seq") * [out_proj], 0),
+                axis_name="seq",
+                split_axis=0,
+                concat_axis=0,
+            ),
+            0,
+        ),
         preferred_element_type=jnp.float32,
     )
     return (projected.astype(jnp.bfloat16), moment_own[None])

time: 360 us -> 328 us (0.911)
  waiting for transfers between devices: 303 us -> 253 us
  starting transfers between devices: 5.49 us -> 22 us
    all_gather x1 -> x0, waiting for transfers between devices: 70.2 us -> none  [shards(): lax.all_gather(out_proj, 'seq', axis=0, tiled=True)]
    psum x1, waiting for transfers between devices: 185 us -> 220 us  [shards(): moment_full = lax.psum(grads + placed, 'seq')]
    all_to_all x0 -> x1, starting transfers between devices: none -> 16.6 us  [shards(): lax.all_to_all(jnp.stack(lax.psum(1, axis_name='seq') * [out_proj], 0), a...]
    ppermute x1, waiting for transfers between devices: 12.2 us -> 0.01 us  [from_behind(): return lax.ppermute(array, axis, pairs)]
  transfers between devices with their start and end apart: 4 -> 4, of which waited for: 4 -> 2; matrix products, arithmetic and copies ran while one was open for 5% -> 9% of each run, Pallas kernels for 0% -> 0%
where the time goes in v1:
time: 328 us
  waiting for transfers between devices  253 us (77%)
  starting transfers between devices  22 us (7%)
  matrix products  20.1 us (6%)
  between operations  14.2 us (4%)
  other arithmetic  12.6 us (4%)
  local copies, waits for them, and re-layouts  5.9 us (2%)
    psum x1, waiting for transfers between devices, shards(): moment_full = lax.psum(grads + placed, 'seq')  220 us
    all_gather x1, waiting for transfers between devices, shards(): all_heads = lax.all_gather(combined, 'head', axis=1, tiled=True)  32.4 us
    all_to_all x1, starting transfers between devices, shards(): lax.all_to_all(jnp.stack(lax.psum(1, axis_name='seq') * [out_proj], 0), a...  16.6 us
    dot_general x5, matrix products, times_transposed(): lax.dot_general(left, right, (((1,), (1,)), ((), ())), preferred_element_...  6.99 us
  transfers between devices with their start and end apart: 4, of which 2 were waited for; matrix products, arithmetic and copies ran while one was open for 9% of the time, Pallas kernels for 0%

profile of v1, /device:TPU:1, one launch (start us, length us, event | category | flops | bytes accessed | tf_op | source)
XLA Modules:
  0.0 327.5 jit_solution(8029557780764490174)
XLA Ops:
  7.2 0.0 copy-start
  7.2 0.0 copy-start.3
  7.2 0.0 copy-start.1
  7.2 0.0 all-reduce.2.cloned.1.call-start
  7.2 2.4 pad_maximum_fusion.1
  9.7 5.4 %collective-permute-start = (bf16[2,512,512]{2,1,0:T(8,128)(2,1)}, bf16[2,512,512]{2,1,0:T(8,128)(2,1)}, u32[]{:S(2)}, u32[]{:S(2)}) collective-permute-start(bf16[2,512,512]{2,1,0:T(8,128)(2,1)} %pad_maximum_fusion.1), channel_id=1, source_target_pairs={{0,4},{4,8},{8,12},{12,16},{16,20},{20,24},{24,28},{28,32},{32,36}... | collective-permute-start | bytes 3145736 | tf_op jit(solution)/shard_map/ppermute | solution.py:17
  15.1 0.0 copy-done.3
  15.1 0.0 copy-done.1
  15.1 0.0 copy-start.11
  15.1 0.0 copy-start.4
  15.1 0.5 fusion.14
  15.6 0.5 fusion.16
  16.0 0.0 copy-done.11
  16.1 0.1 copy-done.4
  16.1 0.5 fusion.18
  16.6 1.6 convolution_bitcast_fusion.2
  18.3 1.8 convolution_bitcast_fusion.4
  20.0 1.5 convolution_bitcast_fusion.3
  21.6 3.9 %pad_maximum_fusion = f32[3,512,512]{2,1,0:T(8,128)} fusion(f32[1,512,512]{2,1,0:T(8,128)} %convolution_bitcast_fusion.2, f32[1,512,512]{2,1,0:T(8,128)} %convolution_bitcast_fusion.3, f32[1,512,512]{2,1,0:T(8,128)} %convolution_bitcast_fusion.4), kind=kLoop, calls=%fused_computation.3 | loop fusion | flops 1572864 | bytes 6291456 | tf_op jit(solution)/shard_map/stack | solution.py:57
  25.4 0.0 copy-done.9
  25.4 1.4 fusion.26
  26.9 0.0 all-reduce.2.cloned.1.call-update
  26.9 0.0 copy-done.10
  26.9 1.6 stack.26
  28.5 16.6 %all-to-all-start = ((bf16[128,16,512]{2,1,0:T(8,128)(2,1)}), bf16[128,16,512]{2,1,0:T(8,128)(2,1)}, u32[]{:S(2)}, u32[]{:S(2)}) async-start(bf16[128,16,512]{2,1,0:T(8,128)(2,1)} %stack.26), calls=%async_computation | async-start | bytes 4194304 | tf_op jit(solution)/shard_map/all_to_all | solution.py:90
  45.1 0.0 all-gather.2.cloned.1.call-start
  45.2 0.0 collective-permute-done
  45.2 1.4 maximum_maximum_fusion
  46.6 0.0 copy-done
  46.6 0.0 copy-start.6
  46.6 1.1 fusion.31
  47.7 0.2 copy-done.6
  47.9 1.3 copy-done.8
  49.2 0.4 fusion.3
  49.6 220.2 %all-reduce.2.cloned.1.call-done = f32[3,512,512]{2,1,0:T(8,128)} async-done(((f32[3,512,512]{2,1,0:T(8,128)}), f32[3,512,512]{2,1,0:T(8,128)}) %all-reduce.2.cloned.1.call-update) | async-done | bytes 3145744 | tf_op jit(solution)/shard_map/psum | solution.py:62
  269.8 2.7 fusion
  272.6 0.1 copy-done.2
  272.6 0.4 multiply_convert_fusion
  273.1 1.2 copy-done.5
  274.2 1.5 convolution_bitcast_fusion.1
  275.7 3.5 %fusion.7 = f32[512,512]{1,0:T(8,128)} fusion(bf16[512,512]{1,0:T(8,128)(2,1)S(1)} %copy-done, f32[512,512]{1,0:T(8,128)} %convolution_bitcast_fusion.1, bf16[3,512,512]{2,1,0:T(8,128)(2,1)} %copy-done.5), kind=kOutput, calls=%fused_computation.25 | convolution fusion | flops 538443776 | bytes 3670016 | tf_op jit(solution)/shard_map/dot_general | solution.py:21
  279.2 0.0 copy-done.7
  279.2 3.4 %fusion.5 = bf16[512,512]{1,0:T(8,128)(2,1)} fusion(f32[512,512]{1,0:T(8,128)} %fusion.7, bf16[2,1024,512]{2,1,0:T(8,128)(2,1)S(1)} %copy-done.7, f32[512,1024]{0,1:T(8,128)} %copy-done.8, f32[512]{0:T(512)S(1)} %fusion.3, f32[512]{0:T(512)S(1)} %get-tuple-element.4), kind=kOutput, calls=%fused_computation.22 | convolution fusion | flops 538968064 | bytes 4722688 | tf_op jit(solution)/shard_map/dot_general | solution.py:84
  282.6 0.0 all-gather.2.cloned.1.call-update
  282.6 1.4 dynamic-slice_bitcast_fusion
  284.0 0.0 all-to-all-done
  284.0 32.4 %all-gather.2.cloned.1.call-done = bf16[512,2048]{1,0:T(8,128)(2,1)} async-done(((bf16[512,512]{1,0:T(8,128)(2,1)}), bf16[512,2048]{1,0:T(8,128)(2,1)}) %all-gather.2.cloned.1.call-update) | async-done | bytes 2097168 | tf_op jit(solution)/shard_map/all_gather | solution.py:86
  316.4 4.3 %convolution_convert_fusion = bf16[512,512]{1,0:T(8,128)(2,1)} fusion(bf16[512,2048]{1,0:T(8,128)(2,1)} %all-gather.2.cloned.1.call-done, bf16[2048,512]{1,0:T(8,128)(2,1)} %bitcast.20), kind=kOutput, calls=%fused_computation.23 | convolution fusion | flops 1074003968 | bytes 4718592 | tf_op jit(solution)/shard_map/dot_general | solution.py:87
  (11 shorter events, 0.0 us)
Async XLA Ops:
  7.2 39.4 %copy-start = (bf16[512,512]{1,0:T(8,128)(2,1)S(1)}, bf16[512,512]{1,0:T(8,128)(2,1)}, u32[]{:S(2)}) copy-start(bf16[512,512]{1,0:T(8,128)(2,1)} %param.7) | copy-start | bytes 1572868
  7.2 7.9 %copy-start.3 = (bf16[512,512]{1,0:T(8,128)(2,1)S(1)}, bf16[512,512]{1,0:T(8,128)(2,1)}, u32[]{:S(2)}) copy-start(bf16[512,512]{1,0:T(8,128)(2,1)} %param.8) | copy-start | bytes 1572868
  7.2 7.9 %copy-start.1 = (bf16[1,3,512,512]{3,2,1,0:T(8,128)(2,1)S(1)}, bf16[1,3,512,512]{3,2,1,0:T(8,128)(2,1)}, u32[]{:S(2)}) copy-start(bf16[1,3,512,512]{3,2,1,0:T(8,128)(2,1)} %param.11) | copy-start | bytes 4718596
  7.2 262.6 %all-reduce.2.cloned.1.call-start = ((), (), s32[]{:S(2)}) async-start(), calls=%async_computation.1 | async-start | bytes 6291456 | tf_op jit(solution)/shard_map/psum | solution.py:62
  9.7 35.5 %collective-permute-start = (bf16[2,512,512]{2,1,0:T(8,128)(2,1)}, bf16[2,512,512]{2,1,0:T(8,128)(2,1)}, u32[]{:S(2)}, u32[]{:S(2)}) collective-permute-start(bf16[2,512,512]{2,1,0:T(8,128)(2,1)} %pad_maximum_fusion.1), channel_id=1, source_target_pairs={{0,4},{4,8},{8,12},{12,16},{16,20},{20,24},{24,28},{28,32},{32,36}... | collective-permute-start | bytes 3145736 | tf_op jit(solution)/shard_map/ppermute | solution.py:17
  15.1 1.0 copy-start.11
  15.1 1.0 copy-start.4
  21.6 3.9 %copy-start.9 = (f32[1,3,4,512]{3,2,1,0:T(4,128)S(1)}, f32[1,3,4,512]{3,2,1,0:T(4,128)}, u32[]{:S(2)}) copy-start(f32[1,3,4,512]{3,2,1,0:T(4,128)} %param.12) | copy-start | bytes 73732
  25.4 1.5 copy-start.10
  28.5 255.5 %all-to-all-start = ((bf16[128,16,512]{2,1,0:T(8,128)(2,1)}), bf16[128,16,512]{2,1,0:T(8,128)(2,1)}, u32[]{:S(2)}, u32[]{:S(2)}) async-start(bf16[128,16,512]{2,1,0:T(8,128)(2,1)} %stack.26), calls=%async_computation | async-start | bytes 4194304 | tf_op jit(solution)/shard_map/all_to_all | solution.py:90
  45.1 271.3 %all-gather.2.cloned.1.call-start = ((), (), s32[]{:S(2)}) async-start(), calls=%async_computation.2 | async-start | bytes 2621440 | tf_op jit(solution)/shard_map/all_gather | solution.py:86
  46.6 1.3 copy-start.6
  47.9 1.3 copy-start.8
  269.8 2.8 copy-start.2
  273.1 1.2 copy-start.5
  275.7 3.5 %copy-start.7 = (bf16[2,1024,512]{2,1,0:T(8,128)(2,1)S(1)}, bf16[2,1024,512]{2,1,0:T(8,128)(2,1)}, u32[]{:S(2)}) copy-start(bf16[2,1024,512]{2,1,0:T(8,128)(2,1)} %copy-done.6) | copy-start | bytes 6291460
Sparse Core Ops, SparseCore 0:
  27.0 242.7 all-reduce.1
  282.7 33.6 all-gather.1
